TPU v7x, 32 devices: a whole 2x2x4 slice. The times are simulated.
32 devices in a mesh: gx: 8 (over y, x, core), pa: 4 (over z).
Axes of the slice: x: 2, y: 2, z: 4, core: 2. Of those that a mesh axis runs over, the one named last changes fastest.
Arguments:
- block_inverses: float32 [32, 32, 128, 128], P('gx', 'pa'), parts along dimension 1, may hold values from -0.25 to 1.07, as said below
- residual: float32 [32, 32, 128], P('gx', 'pa'), parts along dimension 1, may hold values from -0.3 to 0.3
- material: int32 [32, 32, 128], P('gx', 'pa'), parts along dimension 1, may hold values from 0 to 3
- fin_mask: int32 [32, 32, 128], P('gx', 'pa'), parts along dimension 1, may hold values 0 or 1
- phase_mask: int32 [32, 32, 128], P('gx', 'pa'), parts along dimension 1, may hold values 0 or 1
- k_table: float32 [4], replicated, may hold values from 0.95 to 1.05
Outputs:
- correction: float32 [32, 32, 128], P('gx', 'pa'), parts along dimension 1
- enthalpy_step: float32 [32, 32, 128], P('gx', 'pa'), parts along dimension 1
There are 4 independent parts, one for each index of `pa`. A program takes and returns all parts, laid end to end along the dimension named above; an argument that names none is the same for every part. Nothing has to cross between parts.
Inputs may be any that keep to these rules, and one draw needn't show every extreme that they name: Each block block_inverses[i, t] is a symmetric matrix.
All inputs are finite; a program needn't handle non-finite values. No bound on the sum of `fin_mask` or of `phase_mask` on one device may be relied on, other than what follows from the above.
Results may differ from a plain program's by a relative error of at most 0.0003.
Values sent between devices are 32-bit elements; how exact they have to be, the bound alone decides.
No kernel may reach another device: no remote copies, remote signals or barrier semaphores. Data moves between devices by JAX's collectives and lax.ppermute only.
A program may use at most 128 MiB of HBM per device.

v0:
```python
import jax
import jax.numpy as jnp
from jax import lax
from jax.sharding import PartitionSpec as P


def passed_along(block, axis, distance):
    devices = range(lax.axis_size(axis))
    route = [(i - distance, i) for i in devices if i - distance in devices]
    return lax.ppermute(block, axis, route)


def apply_block(pivot_entries, vector):
    return jnp.einsum("tab,tb->ta", pivot_entries, vector, precision=lax.Precision.HIGHEST)


def apply_transposed(pivot_entries, vector):
    return jnp.einsum("tba,tb->ta", pivot_entries, vector, precision=lax.Precision.HIGHEST)


def forward_pass(block_inverses, residual, face_cond, entering):
    state_vec = entering
    results = []
    for line_position in range(block_inverses.shape[0]):
        state_vec = apply_block(
            block_inverses[line_position],
            residual[line_position] + face_cond[line_position] * state_vec,
        )
        results.append(state_vec)
    return jnp.stack(results)


def backward_pass(block_inverses, forward_vals, face_cond, arriving):
    carried = arriving
    results = [None] * block_inverses.shape[0]
    for line_position in reversed(range(block_inverses.shape[0])):
        solved = forward_vals[line_position] + apply_block(block_inverses[line_position], carried)
        results[line_position] = solved
        carried = face_cond[line_position] * solved
    return (jnp.stack(results), carried)


def on_device(block_inverses, residual, material, fin_mask, phase_mask, k_table):
    block_count, tile_count, cell_count = residual.shape
    material_codes = jnp.arange(k_table.shape[0], dtype=jnp.int32)
    conduct = jnp.sum(
        jnp.where(material[..., None] == material_codes, k_table, jnp.zeros_like(k_table)), axis=-1
    )
    before = passed_along(conduct[block_count - 1], "gx", 1)
    earlier = jnp.concatenate([before[None], conduct[: block_count - 1]], axis=0)
    face_cond = (
        2.0 * conduct * earlier / (conduct + earlier) * (0.9 + 0.1 * fin_mask.astype(jnp.float32))
    )
    zero_vector = jnp.zeros((tile_count, cell_count), jnp.float32)
    scaled_rows = block_inverses * face_cond[:, :, None, :]
    matrix_product = scaled_rows[0]
    for line_position in range(1, block_count):
        matrix_product = jnp.einsum(
            "hzp,hpn->hzn",
            scaled_rows[line_position],
            matrix_product,
            precision=lax.Precision.HIGHEST,
        )
    local_vals = forward_pass(block_inverses, residual, face_cond, zero_vector)
    tail_vec = local_vals[block_count - 1]
    all_maps, all_tails = (
        lax.all_gather(matrix_product[None], "gx", axis=0, tiled=True),
        lax.all_gather(tail_vec[None], "gx", axis=0, tiled=True),
    )
    own_index = lax.axis_index("gx")
    processor_total = all_maps.shape[0]

    def fold_forward(line_position, state_vec):
        moved = apply_block(all_maps[line_position], state_vec) + all_tails[line_position]
        return jnp.where(line_position < own_index, moved, state_vec)

    entering = lax.fori_loop(0, processor_total, fold_forward, zero_vector, unroll=8)
    forward_vals = forward_pass(block_inverses, residual, face_cond, entering)
    _, leaving = backward_pass(block_inverses, forward_vals, face_cond, zero_vector)
    all_leaving = lax.all_gather(leaving[None], "gx", axis=0, tiled=True)

    def backward_accumulate(offset, state_vec):
        line_position = processor_total - 1 - offset
        moved = apply_transposed(all_maps[line_position], state_vec) + all_leaving[line_position]
        return jnp.where(line_position > own_index, moved, state_vec)

    arriving = lax.fori_loop(0, processor_total, backward_accumulate, zero_vector, unroll=8)
    correction, _ = backward_pass(block_inverses, forward_vals, face_cond, arriving)
    enthalpy_step = correction * (1.0 + 2.0 * phase_mask.astype(jnp.float32))
    return (correction, enthalpy_step)


def solution(mesh):
    return jax.shard_map(
        on_device,
        mesh=mesh,
        in_specs=(
            P("gx", "pa", None, None),
            P("gx", "pa", None),
            P("gx", "pa", None),
            P("gx", "pa", None),
            P("gx", "pa", None),
            P(),
        ),
        out_specs=(P("gx", "pa", None), P("gx", "pa", None)),
        check_vma=False,
    )
```

profile of v0, /device:TPU:0, one launch (start us, length us, event | category | flops | bytes accessed | tf_op | source)
XLA Modules:
  0.0 100.5 jit_solution(474527091113292094)
XLA Ops:
  7.2 0.0 all-gather.5.cloned.1.call-start
  7.2 0.8 select_reduce_fusion
  8.0 2.3 %collective-permute-start = (f32[8,128]{1,0:T(8,128)S(1)}, f32[8,128]{1,0:T(8,128)S(1)}, u32[]{:S(2)}, u32[]{:S(2)}) collective-permute-start(f32[8,128]{1,0:T(8,128)S(1)} %slice_bitcast_fusion.12), channel_id=1, source_target_pairs={{0,4},{4,8},{8,12},{12,16},{16,20},{20,24},{24,28},{1,5},{5,9},{9,... | collective-permute-start | bytes 12296 | tf_op jit(solution)/shard_map/ppermute | solution.py:10
  10.4 0.8 collective-permute-done
  11.2 0.7 add_multiply_fusion.1
  11.9 0.0 copy-start.1
  11.9 0.0 copy-start.2
  11.9 1.9 %broadcast_multiply_fusion = f32[4,8,128,128]{3,2,1,0:T(8,128)S(1)} fusion(f32[4,8,128,128]{3,2,1,0:T(8,128)} %param.6, f32[4,8,128]{2,1,0:T(8,128)S(1)} %add_multiply_fusion.1), kind=kLoop, calls=%fused_computation | loop fusion | flops 524288 | bytes 4210688 | tf_op jit(solution)/shard_map/mul | solution.py:55
  13.9 0.7 fusion
  14.5 0.7 fusion.1
  15.2 1.5 %fusion.2 = f32[8,128,128]{2,1,0:T(8,128)} fusion(f32[8,128,128]{2,1,0:T(8,128)S(1)} %fusion.1, f32[4,8,128,128]{3,2,1,0:T(8,128)S(1)} %broadcast_multiply_fusion), kind=kOutput, calls=%fused_computation.7 | convolution fusion | flops 201326592 | bytes 1572864 | tf_op jit(solution)/shard_map/hzp,hpn->hzn/dot_general | solution.py:58
  16.7 0.0 all-gather.5.cloned.1.call-update
  16.8 0.0 copy-done.1
  16.8 0.9 fusion.5
  17.7 0.0 copy-done.2
  17.7 0.9 fusion.33
  18.6 0.9 fusion.25
  19.6 1.0 fusion.17
  20.5 0.9 fusion.9
  21.5 13.4 %all-gather.1 = f32[64,128]{1,0:T(8,128)S(1)} all-gather(f32[8,128]{1,0:T(8,128)S(1)} %bitcast.349), channel_id=3, replica_groups=mesh['gx'=8,'pa'=4] {'gx'}, dimensions={0}, use_global_device_ids=true | all-gather | bytes 36864 | tf_op jit(solution)/shard_map/all_gather | solution.py:68
  34.8 23.2 %all-gather.5.cloned.1.call-done = f32[64,128,128]{2,1,0:T(8,128)} async-done(((f32[8,128,128]{2,1,0:T(8,128)}), f32[64,128,128]{2,1,0:T(8,128)}) %all-gather.5.cloned.1.call-update) | async-done | bytes 4194320 | tf_op jit(solution)/shard_map/all_gather | solution.py:67
  58.0 0.0 copy-start
  58.0 2.1 %fusion.72 = f32[8,1,128]{2,1,0:T(1,128)S(1)} fusion(f32[64,128,128]{2,1,0:T(8,128)} %all-gather.5.cloned.1.call-done, f32[8,128,1]{1,2,0:T(1,128)S(1)} %bitcast.312), kind=kOutput, calls=%fused_computation.119 | convolution fusion | flops 1572864 | bytes 4202496 | tf_op jit(solution)/shard_map/eval_jaxpr/tab,tb->ta/dot_general | solution.py:14
  60.1 2.0 %fusion.73 = f32[8,1,128]{2,1,0:T(1,128)S(1)} fusion(f32[64,128,128]{2,1,0:T(8,128)} %all-gather.5.cloned.1.call-done, f32[8,128,1]{1,2,0:T(1,128)S(1)} %bitcast.326), kind=kOutput, calls=%fused_computation.120 | convolution fusion | flops 1572864 | bytes 4202496 | tf_op jit(solution)/shard_map/eval_jaxpr/tab,tb->ta/dot_general | solution.py:14
  62.1 2.0 %fusion.74 = f32[8,1,128]{2,1,0:T(1,128)S(1)} fusion(f32[64,128,128]{2,1,0:T(8,128)} %all-gather.5.cloned.1.call-done, f32[8,128,1]{1,2,0:T(1,128)S(1)} %bitcast.329), kind=kOutput, calls=%fused_computation.121 | convolution fusion | flops 1572864 | bytes 4202496 | tf_op jit(solution)/shard_map/eval_jaxpr/tab,tb->ta/dot_general | solution.py:14
  64.1 0.0 copy-done
  64.1 0.9 fusion.75
  65.0 0.9 fusion.76
  66.0 0.9 fusion.77
  66.9 0.9 fusion.78
  67.9 0.9 fusion.79
  68.8 0.9 fusion.31
  69.7 0.9 fusion.23
  70.7 0.9 fusion.15
  71.6 0.9 fusion.7
  72.6 0.9 fusion.13
  73.5 0.9 fusion.21
  74.5 0.9 fusion.29
  75.4 9.2 %all-gather.2 = f32[64,128]{1,0:T(8,128)S(1)} all-gather(f32[8,128]{1,0:T(8,128)S(1)} %add_multiply_fusion.2), channel_id=4, replica_groups=mesh['gx'=8,'pa'=4] {'gx'}, dimensions={0}, use_global_device_ids=true | all-gather | bytes 36864 | tf_op jit(solution)/shard_map/all_gather | solution.py:80
  84.7 0.5 fusion.80
  85.2 0.6 fusion.81
  85.8 0.6 fusion.82
  86.4 0.6 fusion.83
  86.9 0.0 copy-start.3
  86.9 0.6 fusion.84
  87.5 0.6 fusion.85
  88.1 0.6 fusion.86
  88.6 0.6 fusion.87
  89.2 0.9 fusion.3
  90.2 0.9 fusion.11
  91.1 0.9 fusion.19
  92.0 0.9 fusion.27
  93.0 0.0 copy-done.3
  93.0 0.6 add_multiply_fusion
  (34 shorter events, 0.2 us)
Async XLA Ops:
  7.2 50.9 %all-gather.5.cloned.1.call-start = ((), (), s32[]{:S(2)}) async-start(), calls=%async_computation | async-start | bytes 4718592 | tf_op jit(solution)/shard_map/all_gather | solution.py:67
  8.0 3.2 %collective-permute-start = (f32[8,128]{1,0:T(8,128)S(1)}, f32[8,128]{1,0:T(8,128)S(1)}, u32[]{:S(2)}, u32[]{:S(2)}) collective-permute-start(f32[8,128]{1,0:T(8,128)S(1)} %slice_bitcast_fusion.12), channel_id=1, source_target_pairs={{0,4},{4,8},{8,12},{12,16},{16,20},{20,24},{24,28},{1,5},{5,9},{9,... | collective-permute-start | bytes 12296 | tf_op jit(solution)/shard_map/ppermute | solution.py:10
  11.9 4.8 %copy-start.1 = (f32[4,8,128,128]{3,2,1,0:T(8,128)S(1)}, f32[4,8,128,128]{3,2,1,0:T(8,128)}, u32[]{:S(2)}) copy-start(f32[4,8,128,128]{3,2,1,0:T(8,128)} %param.6) | copy-start | bytes 6291460
  11.9 5.8 %copy-start.2 = (f32[4,8,128]{2,1,0:T(8,128)S(1)}, f32[4,8,128]{2,1,0:T(8,128)}, u32[]{:S(2)}) copy-start(f32[4,8,128]{2,1,0:T(8,128)} %param.7) | copy-start | bytes 49156
  58.0 6.1 %copy-start = (f32[64,128,128]{2,1,0:T(8,128)S(1)}, f32[64,128,128]{2,1,0:T(8,128)}, u32[]{:S(2)}) copy-start(f32[64,128,128]{2,1,0:T(8,128)} %all-gather.5.cloned.1.call-done) | copy-start | bytes 12582916
  86.9 6.1 %copy-start.3 = (s32[4,8,128]{2,1,0:T(8,128)S(1)}, s32[4,8,128]{2,1,0:T(8,128)}, u32[]{:S(2)}) copy-start(s32[4,8,128]{2,1,0:T(8,128)} %param.10) | copy-start | bytes 49156
Sparse Core Ops, SparseCore 0:
  16.8 41.1 all-gather.4
where the time goes:
time: 101 us; the launch traced here: 100 us
  matrix products  32.9 us (33%)
  waiting for transfers between devices  24 us (24%)
  blocking collectives  22.6 us (22%)
  between operations  14.2 us (14%)
  other arithmetic  4.31 us (4%)
  starting transfers between devices  2.38 us (2%)
    dot_general x24, matrix products, apply_block(): jnp.einsum('tab,tb->ta', pivot_entries, vector, precision=lax.Precision.H...  25.7 us
    all_gather x1, waiting for transfers between devices, on_device(): lax.all_gather(matrix_product[None], 'gx', axis=0, tiled=True)  23.2 us
    all_gather x1, blocking collectives, on_device(): lax.all_gather(tail_vec[None], 'gx', axis=0, tiled=True)  13.4 us
    all_gather x1, blocking collectives, on_device(): all_leaving = lax.all_gather(leaving[None], 'gx', axis=0, tiled=True)  9.25 us
    dot_general x8, matrix products, apply_transposed(): jnp.einsum('tba,tb->ta', pivot_entries, vector, precision=lax.Precision.H...  4.48 us
    dot_general x3, matrix products, on_device(): jnp.einsum('hzp,hpn->hzn', scaled_rows[line_position], matrix_product, pr...  2.81 us
    ppermute x1, starting transfers between devices, passed_along(): return lax.ppermute(block, axis, route)  2.35 us
  transfers between devices with their start and end apart: 2, of which 2 were waited for; matrix products, arithmetic and copies ran while one was open for 5% of the time, Pallas kernels for 0%

commit v1 on v0

--- a/solution.py
+++ b/solution.py
@@ -2,6 +2,18 @@
 import jax.numpy as jnp
 from jax import lax
 from jax.sharding import PartitionSpec as P
+
+
+def doubled_up(value, axis, dim):
+    ways, here = (lax.axis_size(axis), lax.axis_index(axis))
+    grown, reach = (value, 1)
+    while reach < ways:
+        theirs = lax.ppermute(grown, axis, [(d, d ^ reach) for d in range(ways)])
+        mine_first = jnp.concatenate([grown, theirs], axis=dim)
+        theirs_first = jnp.concatenate([theirs, grown], axis=dim)
+        grown = jnp.where(here & reach == 0, mine_first, theirs_first)
+        reach = 2 * reach
+    return grown
 
 
 def passed_along(block, axis, distance):
@@ -64,7 +76,7 @@
     local_vals = forward_pass(block_inverses, residual, face_cond, zero_vector)
     tail_vec = local_vals[block_count - 1]
     all_maps, all_tails = (
-        lax.all_gather(matrix_product[None], "gx", axis=0, tiled=True),
+        doubled_up(matrix_product[None], "gx", 0),
         lax.all_gather(tail_vec[None], "gx", axis=0, tiled=True),
     )
     own_index = lax.axis_index("gx")

time: 101 us -> 131 us (1.30)
  blocking collectives: 22.6 us -> 53.5 us
  between operations: 14.2 us -> 0.74 us
  starting transfers between devices: 2.38 us -> 10.2 us
  other arithmetic: 4.31 us -> 11.6 us
  matrix products: 32.9 us -> 28.9 us
  waiting for transfers between devices: 24 us -> 25.9 us
    all_gather x1, blocking collectives: 13.4 us -> 44.2 us  [on_device(): lax.all_gather(tail_vec[None], 'gx', axis=0, tiled=True)]
    ppermute x0 -> x3, waiting for transfers between devices: none -> 25.1 us  [doubled_up(): theirs = lax.ppermute(grown, axis, [(d, d ^ reach) for d in range(ways)])]
    all_gather x1 -> x0, waiting for transfers between devices: 23.2 us -> none  [on_device(): lax.all_gather(matrix_product[None], 'gx', axis=0, tiled=True)]
    ppermute x0 -> x3, starting transfers between devices: none -> 7.86 us  [doubled_up(): theirs = lax.ppermute(grown, axis, [(d, d ^ reach) for d in range(ways)])]
    select_n x0 -> x3, other arithmetic: none -> 7.42 us  [doubled_up(): grown = jnp.where(here & reach == 0, mine_first, theirs_first)]
    dot_general x24, matrix products: 25.7 us -> 22.4 us  [apply_block(): jnp.einsum('tab,tb->ta', pivot_entries, vector, precision=lax.Precision.H...]
  transfers between devices with their start and end apart: 2 -> 4, of which waited for: 2 -> 3; matrix products, arithmetic and copies ran while one was open for 5% -> 4% of each run, Pallas kernels for 0% -> 0%
where the time goes in v1:
time: 131 us
  blocking collectives  53.5 us (41%)
  matrix products  28.9 us (22%)
  waiting for transfers between devices  25.9 us (20%)
  other arithmetic  11.6 us (9%)
  starting transfers between devices  10.2 us (8%)
    all_gather x1, blocking collectives, on_device(): lax.all_gather(tail_vec[None], 'gx', axis=0, tiled=True)  44.2 us
    ppermute x3, waiting for transfers between devices, doubled_up(): theirs = lax.ppermute(grown, axis, [(d, d ^ reach) for d in range(ways)])  25.1 us
    dot_general x24, matrix products, apply_block(): jnp.einsum('tab,tb->ta', pivot_entries, vector, precision=lax.Precision.H...  22.4 us
    all_gather x1, blocking collectives, on_device(): all_leaving = lax.all_gather(leaving[None], 'gx', axis=0, tiled=True)  9.3 us
    ppermute x3, starting transfers between devices, doubled_up(): theirs = lax.ppermute(grown, axis, [(d, d ^ reach) for d in range(ways)])  7.86 us
    select_n x3, other arithmetic, doubled_up(): grown = jnp.where(here & reach == 0, mine_first, theirs_first)  7.42 us
    dot_general x8, matrix products, apply_transposed(): jnp.einsum('tba,tb->ta', pivot_entries, vector, precision=lax.Precision.H...  4.49 us
  transfers between devices with their start and end apart: 4, of which 3 were waited for; matrix products, arithmetic and copies ran while one was open for 4% of the time, Pallas kernels for 0%

profile of v1, /device:TPU:0, one launch (start us, length us, event | category | flops | bytes accessed | tf_op | source)
XLA Modules:
  0.0 130.8 jit_solution(9764391191305653658)
XLA Ops:
  0.6 0.8 select_reduce_fusion
  1.4 2.3 %collective-permute-start = (f32[8,128]{1,0:T(8,128)S(1)}, f32[8,128]{1,0:T(8,128)S(1)}, u32[]{:S(2)}, u32[]{:S(2)}) collective-permute-start(f32[8,128]{1,0:T(8,128)S(1)} %slice_bitcast_fusion.36), channel_id=1, source_target_pairs={{0,4},{4,8},{8,12},{12,16},{16,20},{20,24},{24,28},{1,5},{5,9},{9,... | collective-permute-start | bytes 12296 | tf_op jit(solution)/shard_map/ppermute | solution.py:22
  3.8 0.8 collective-permute-done
  4.6 0.7 add_multiply_fusion.1
  5.3 1.8 %broadcast_multiply_fusion = f32[4,8,128,128]{3,2,1,0:T(8,128)S(1)} fusion(f32[4,8,128,128]{3,2,1,0:T(8,128)} %param.6, f32[4,8,128]{2,1,0:T(8,128)S(1)} %add_multiply_fusion.1), kind=kLoop, calls=%fused_computation.4 | loop fusion | flops 524288 | bytes 4210688 | tf_op jit(solution)/shard_map/mul | solution.py:67
  7.1 0.7 fusion
  7.8 0.7 fusion.1
  8.5 0.7 convolution_bitcast_fusion
  9.1 2.6 %collective-permute-start.1 = (f32[1,8,128,128]{3,2,1,0:T(8,128)S(1)}, f32[1,8,128,128]{3,2,1,0:T(8,128)S(1)}, u32[]{:S(2)}, u32[]{:S(2)}) collective-permute-start(f32[1,8,128,128]{3,2,1,0:T(8,128)S(1)} %convolution_bitcast_fusion), channel_id=1, source_target_pairs={{0,4},{4,0},{8,12},{12,8},{16,20},{20,16},{24,28},{28,24},{1,5},{5... | collective-permute-start | bytes 1572872 | tf_op jit(solution)/shard_map/ppermute | solution.py:11
  11.7 1.5 %collective-permute-done.1 = f32[1,8,128,128]{3,2,1,0:T(8,128)S(1)} collective-permute-done((f32[1,8,128,128]{3,2,1,0:T(8,128)S(1)}, f32[1,8,128,128]{3,2,1,0:T(8,128)S(1)}, u32[]{:S(2)}, u32[]{:S(2)}) %collective-permute-start.1) | collective-permute-done | bytes 524320 | tf_op jit(solution)/shard_map/ppermute | solution.py:11
  13.3 0.1 maximum_select_fusion.2
  13.4 2.6 %collective-permute-start.2 = (f32[2,8,128,128]{3,2,1,0:T(8,128)S(1)}, f32[2,8,128,128]{3,2,1,0:T(8,128)}, u32[]{:S(2)}, u32[]{:S(2)}) collective-permute-start(f32[2,8,128,128]{3,2,1,0:T(8,128)S(1)} %maximum_select_fusion.2), channel_id=1, source_target_pairs={{0,8},{4,12},{8,0},{12,4},{16,24},{20,28},{24,16},{28,20},{1,9},{5... | collective-permute-start | bytes 3145736 | tf_op jit(solution)/shard_map/ppermute | solution.py:11
  16.0 0.0 copy-start
  16.0 0.0 copy-start.1
  16.0 23.6 %collective-permute-done.2 = f32[2,8,128,128]{3,2,1,0:T(8,128)} collective-permute-done((f32[2,8,128,128]{3,2,1,0:T(8,128)S(1)}, f32[2,8,128,128]{3,2,1,0:T(8,128)}, u32[]{:S(2)}, u32[]{:S(2)}) %collective-permute-start.2) | collective-permute-done | bytes 1048608 | tf_op jit(solution)/shard_map/ppermute | solution.py:11
  39.5 3.1 %maximum_select_fusion.1 = f32[4,8,128,128]{3,2,1,0:T(8,128)} fusion(f32[2,8,128,128]{3,2,1,0:T(8,128)} %collective-permute-done.2, f32[2,8,128,128]{3,2,1,0:T(8,128)S(1)} %maximum_select_fusion.2, pred[]{:T(512)S(6)} %eq.26), kind=kLoop, calls=%fused_computation.1 | loop fusion | flops 1572864 | bytes 4194305 | tf_op jit(solution)/shard_map/jit(_where)/select_n | solution.py:14
  42.6 2.7 %collective-permute-start.3 = (f32[4,8,128,128]{3,2,1,0:T(8,128)}, f32[4,8,128,128]{3,2,1,0:T(8,128)}, u32[]{:S(2)}, u32[]{:S(2)}) collective-permute-start(f32[4,8,128,128]{3,2,1,0:T(8,128)} %maximum_select_fusion.1), channel_id=1, source_target_pairs={{0,16},{4,20},{8,24},{12,28},{16,0},{20,4},{24,8},{28,12},{1,17},{... | collective-permute-start | bytes 6291464 | tf_op jit(solution)/shard_map/ppermute | solution.py:11
  45.3 0.0 copy-done
  45.3 0.9 fusion.4
  46.2 0.0 copy-done.1
  46.2 0.9 fusion.32
  47.2 0.9 fusion.24
  48.1 0.9 fusion.16
  49.1 0.9 fusion.8
  50.0 44.2 %all-gather = f32[64,128]{1,0:T(8,128)S(1)} all-gather(f32[8,128]{1,0:T(8,128)S(1)} %bitcast.368), channel_id=2, replica_groups=mesh['gx'=8,'pa'=4] {'gx'}, dimensions={0}, use_global_device_ids=true | all-gather | bytes 36864 | tf_op jit(solution)/shard_map/all_gather | solution.py:80
  94.2 0.0 collective-permute-done.3
  94.2 4.2 %maximum_select_fusion = f32[8,8,128,128]{3,2,1,0:T(8,128)S(1)} fusion(f32[4,8,128,128]{3,2,1,0:T(8,128)} %collective-permute-done.3, f32[4,8,128,128]{3,2,1,0:T(8,128)} %maximum_select_fusion.1, pred[]{:T(512)S(6)} %eq.25), kind=kLoop, calls=%fused_computation | loop fusion | flops 3145728 | bytes 8388609 | tf_op jit(solution)/shard_map/jit(_where)/select_n | solution.py:14
  98.4 0.9 fusion.49
  99.3 0.6 fusion.34
  99.9 0.9 fusion.47
  100.8 0.9 fusion.45
  101.8 0.9 fusion.43
  102.7 0.9 fusion.41
  103.7 0.9 fusion.39
  104.6 0.9 fusion.37
  105.5 0.9 fusion.35
  106.5 0.9 fusion.30
  107.4 0.9 fusion.22
  108.4 0.9 fusion.14
  109.3 0.9 fusion.6
  110.3 0.9 fusion.12
  111.2 0.9 fusion.20
  112.2 0.9 fusion.28
  113.1 9.3 %all-gather.1 = f32[64,128]{1,0:T(8,128)S(1)} all-gather(f32[8,128]{1,0:T(8,128)S(1)} %add_multiply_fusion.2), channel_id=3, replica_groups=mesh['gx'=8,'pa'=4] {'gx'}, dimensions={0}, use_global_device_ids=true | all-gather | bytes 36864 | tf_op jit(solution)/shard_map/all_gather | solution.py:92
  122.4 0.6 fusion.36
  123.0 0.6 fusion.38
  123.6 0.6 fusion.40
  124.1 0.0 copy-start.2
  124.1 0.6 fusion.42
  124.7 0.6 fusion.44
  125.3 0.6 fusion.46
  125.8 0.6 fusion.48
  126.4 0.9 fusion.2
  127.3 0.9 fusion.10
  128.3 0.9 fusion.18
  129.2 0.9 fusion.26
  130.2 0.0 copy-done.2
  130.2 0.6 add_multiply_fusion
  (34 shorter events, 0.2 us)
Async XLA Ops:
  1.4 3.2 %collective-permute-start = (f32[8,128]{1,0:T(8,128)S(1)}, f32[8,128]{1,0:T(8,128)S(1)}, u32[]{:S(2)}, u32[]{:S(2)}) collective-permute-start(f32[8,128]{1,0:T(8,128)S(1)} %slice_bitcast_fusion.36), channel_id=1, source_target_pairs={{0,4},{4,8},{8,12},{12,16},{16,20},{20,24},{24,28},{1,5},{5,9},{9,... | collective-permute-start | bytes 12296 | tf_op jit(solution)/shard_map/ppermute | solution.py:22
  9.1 4.1 %collective-permute-start.1 = (f32[1,8,128,128]{3,2,1,0:T(8,128)S(1)}, f32[1,8,128,128]{3,2,1,0:T(8,128)S(1)}, u32[]{:S(2)}, u32[]{:S(2)}) collective-permute-start(f32[1,8,128,128]{3,2,1,0:T(8,128)S(1)} %convolution_bitcast_fusion), channel_id=1, source_target_pairs={{0,4},{4,0},{8,12},{12,8},{16,20},{20,16},{24,28},{28,24},{1,5},{5... | collective-permute-start | bytes 1572872 | tf_op jit(solution)/shard_map/ppermute | solution.py:11
  13.4 26.2 %collective-permute-start.2 = (f32[2,8,128,128]{3,2,1,0:T(8,128)S(1)}, f32[2,8,128,128]{3,2,1,0:T(8,128)}, u32[]{:S(2)}, u32[]{:S(2)}) collective-permute-start(f32[2,8,128,128]{3,2,1,0:T(8,128)S(1)} %maximum_select_fusion.2), channel_id=1, source_target_pairs={{0,8},{4,12},{8,0},{12,4},{16,24},{20,28},{24,16},{28,20},{1,9},{5... | collective-permute-start | bytes 3145736 | tf_op jit(solution)/shard_map/ppermute | solution.py:11
  16.0 29.3 %copy-start = (f32[4,8,128,128]{3,2,1,0:T(8,128)S(1)}, f32[4,8,128,128]{3,2,1,0:T(8,128)}, u32[]{:S(2)}) copy-start(f32[4,8,128,128]{3,2,1,0:T(8,128)} %param.6) | copy-start | bytes 6291460
  16.0 30.3 %copy-start.1 = (f32[4,8,128]{2,1,0:T(8,128)S(1)}, f32[4,8,128]{2,1,0:T(8,128)}, u32[]{:S(2)}) copy-start(f32[4,8,128]{2,1,0:T(8,128)} %param.7) | copy-start | bytes 49156
  42.6 51.5 %collective-permute-start.3 = (f32[4,8,128,128]{3,2,1,0:T(8,128)}, f32[4,8,128,128]{3,2,1,0:T(8,128)}, u32[]{:S(2)}, u32[]{:S(2)}) collective-permute-start(f32[4,8,128,128]{3,2,1,0:T(8,128)} %maximum_select_fusion.1), channel_id=1, source_target_pairs={{0,16},{4,20},{8,24},{12,28},{16,0},{20,4},{24,8},{28,12},{1,17},{... | collective-permute-start | bytes 6291464 | tf_op jit(solution)/shard_map/ppermute | solution.py:11
  124.1 6.1 %copy-start.2 = (s32[4,8,128]{2,1,0:T(8,128)S(1)}, s32[4,8,128]{2,1,0:T(8,128)}, u32[]{:S(2)}) copy-start(s32[4,8,128]{2,1,0:T(8,128)} %param.10) | copy-start | bytes 49156
